TPU v7x, 512 devices: a whole 4x8x8 slice. The times are simulated.
512 devices in a mesh: dp: 16 (over y, core), tensor: 32 (over z, x).
Axes of the slice: x: 4, y: 8, z: 8, core: 2. Of those that a mesh axis runs over, the one named last changes fastest.
Arguments:
- tokens: bfloat16 [5632, 4096], P('dp', 'tensor'), may hold values from -6 to 6
- grad_out: bfloat16 [5632, 4096], P('dp', 'tensor'), may hold values from -6 to 6
- routes: float32 [16, 2, 16], P('dp'), may hold values from 0.005 to 0.3
- counts: int32 [16], P('dp'), may hold values from 176 to 352
- up_weight: bfloat16 [16, 4096, 4096], P(None, 'dp', 'tensor'), may hold values from -0.09375 to 0.09375
- down_weight: bfloat16 [16, 4096, 4096], P(None, 'tensor', 'dp'), may hold values from -0.09375 to 0.09375
Outputs:
- input_grad: bfloat16 [5632, 4096], P('dp', 'tensor')
- up_grad: bfloat16 [16, 4096, 4096], P(None, 'dp', 'tensor')
- down_grad: bfloat16 [16, 4096, 4096], P(None, 'tensor', 'dp')
- route_grad: float32 [16, 2, 16], P('dp')
Inputs may be any that keep to these rules, and one draw needn't show every extreme that they name: `counts`: the valid tokens of a data group, at least one whole segment.
All inputs are finite; a program needn't handle non-finite values.
Results may differ from a plain program's by a relative error of at most 0.02.
Values may be sent and summed in bfloat16 or wider, within the bound.
No kernel may reach another device: no remote copies, remote signals or barrier semaphores. Data moves between devices by JAX's collectives and lax.ppermute only.
A program may use at most 64 MiB of HBM per device.

v0:
```python
import jax
import jax.numpy as jnp
from jax import lax
from jax.sharding import PartitionSpec as P

gelu_scale = 0.7978845608
gelu_cubic = 0.044715


def gelu_pair(inputs):
    inner = gelu_scale * (inputs + gelu_cubic * inputs * inputs * inputs)
    tangent = jnp.tanh(inner)
    activated = 0.5 * inputs * (1.0 + tangent)
    derivative = 0.5 * (1.0 + tangent) + 0.5 * inputs * (1.0 - tangent * tangent) * gelu_scale * (
        1.0 + 3.0 * gelu_cubic * inputs * inputs
    )
    return (activated, derivative)


def body(tokens, grad_out, routes, counts, up_weight, down_weight):
    group_rows = tokens.shape[0]
    experts = up_weight.shape[0]
    segments = routes.shape[1]
    seg_rows = group_rows // segments
    high = lax.Precision.HIGHEST
    valid = (jnp.arange(group_rows, dtype=jnp.int32) < counts[0])[:, None]
    masked = jnp.where(valid, grad_out, jnp.zeros_like(grad_out))
    full_tokens, full_grads = (
        lax.all_gather(tokens, "tensor", axis=1, tiled=True),
        lax.all_gather(masked, "tensor", axis=1, tiled=True),
    )
    all_routes = lax.all_gather(routes, "dp", axis=0, tiled=True)
    flat_routes = all_routes.reshape(-1, experts)
    local_up = jnp.dot(
        flat_routes, up_weight.reshape(experts, -1).astype(jnp.float32), precision=high
    )
    local_up = local_up.reshape((-1,) + up_weight.shape[1:]).astype(jnp.bfloat16)
    down_turned = jnp.swapaxes(down_weight, 1, 2)
    local_down = jnp.dot(
        flat_routes, down_turned.reshape(experts, -1).astype(jnp.float32), precision=high
    )
    local_down = local_down.reshape((-1,) + down_turned.shape[1:]).astype(jnp.bfloat16)
    merged_up, merged_down = (
        lax.all_to_all(local_up, "dp", split_axis=0, concat_axis=1, tiled=True),
        lax.all_to_all(local_down, "dp", split_axis=0, concat_axis=1, tiled=True),
    )
    down_terms = []
    slopes = []
    for segment in range(segments):
        seg_tokens = full_tokens[segment * seg_rows : (segment + 1) * seg_rows]
        seg_grads = full_grads[segment * seg_rows : (segment + 1) * seg_rows]
        pre = jnp.dot(seg_tokens, merged_up[segment], preferred_element_type=jnp.float32)
        activated, derivative = gelu_pair(pre)
        activated = activated.astype(jnp.bfloat16)
        slopes.append(derivative)
        down_terms.append(
            jnp.einsum(
                "rd,rh->dh", seg_grads, activated, preferred_element_type=jnp.float32
            ).astype(jnp.bfloat16)
        )
    down_stack = jnp.stack(down_terms, axis=0)
    up_terms = []
    hidden_grads = []
    for segment in range(segments):
        seg_tokens = full_tokens[segment * seg_rows : (segment + 1) * seg_rows]
        seg_grads = full_grads[segment * seg_rows : (segment + 1) * seg_rows]
        back = jnp.einsum(
            "rd,dh->rh", seg_grads, merged_down[segment], preferred_element_type=jnp.float32
        )
        hidden_grad = (back * slopes[segment]).astype(jnp.bfloat16)
        hidden_grads.append(hidden_grad)
        up_terms.append(
            jnp.einsum(
                "rd,rh->dh", seg_tokens, hidden_grad, preferred_element_type=jnp.float32
            ).astype(jnp.bfloat16)
        )
    up_stack = jnp.stack(up_terms, axis=0)
    recv_up, recv_down = (
        lax.all_to_all(up_stack, "dp", split_axis=1, concat_axis=0, tiled=True),
        lax.all_to_all(down_stack, "dp", split_axis=1, concat_axis=0, tiled=True),
    )
    partials = [
        jnp.einsum(
            "rh,dh->rd",
            hidden_grads[segment],
            merged_up[segment],
            preferred_element_type=jnp.float32,
        )
        for segment in range(segments)
    ]
    rounded = lax.optimization_barrier(jnp.concatenate(partials, axis=0).astype(jnp.bfloat16))
    summed = lax.psum_scatter(
        rounded.astype(jnp.float32).astype(jnp.bfloat16), "tensor", scatter_dimension=1, tiled=True
    )
    up_grad = jnp.einsum(
        "ke,kdh->edh", flat_routes, recv_up.astype(jnp.float32), precision=high
    ).astype(jnp.bfloat16)
    down_grad = jnp.einsum(
        "ke,kdh->ehd", flat_routes, recv_down.astype(jnp.float32), precision=high
    ).astype(jnp.bfloat16)
    inner_sums = jnp.einsum("kdh,edh->ke", recv_up, up_weight, preferred_element_type=jnp.float32)
    inner_sums = inner_sums + jnp.einsum(
        "kdh,ehd->ke", recv_down, down_weight, preferred_element_type=jnp.float32
    )
    table = inner_sums.reshape(all_routes.shape)
    totals = lax.psum(table, ("dp", "tensor"))
    route_grad = lax.dynamic_slice_in_dim(totals, lax.axis_index("dp"), 1, 0)
    return (summed, up_grad, down_grad, route_grad)


def solution(mesh):
    return jax.shard_map(
        body,
        mesh=mesh,
        in_specs=(
            P("dp", "tensor"),
            P("dp", "tensor"),
            P("dp", None, None),
            P("dp"),
            P(None, "dp", "tensor"),
            P(None, "tensor", "dp"),
        ),
        out_specs=(
            P("dp", "tensor"),
            P(None, "dp", "tensor"),
            P(None, "tensor", "dp"),
            P("dp", None, None),
        ),
        check_vma=False,
    )
```

profile of v0, /device:TPU:8, one launch (start us, length us, event | category | flops | bytes accessed | tf_op | source)
XLA Modules:
  0.0 445.9 jit_solution(14864564712320135347)
XLA Ops:
  7.9 20.2 %all_gather.10 = f32[16,2,16]{2,1,0:T(2,128)S(1)} all-gather(f32[1,2,16]{2,1,0:T(2,128)} %param.8), channel_id=1, replica_groups=mesh['dp'=16,'tensor'=32] {'dp'}, dimensions={0}, use_global_device_ids=true | all-gather | bytes 2176 | tf_op jit(solution)/shard_map/all_gather | solution.py:32
  28.1 3.1 convolution_convert_fusion.6
  31.2 2.2 copy.65
  33.4 3.8 all-to-all-start.1
  40.2 1.9 convolution_convert_fusion.7
  42.1 2.2 copy.62
  44.3 40.2 %all-to-all-done.1 = bf16[32,256,128]{2,1,0:T(8,128)(2,1)S(1)} async-done(((bf16[32,256,128]{2,1,0:T(8,128)(2,1)}), bf16[32,256,128]{2,1,0:T(8,128)(2,1)S(1)}, u32[]{:S(2)}, u32[]{:S(2)}) %all-to-all-start.1) | async-done | bytes 2097184 | tf_op jit(solution)/shard_map/all_to_all | solution.py:44
  84.5 6.6 %all-to-all-start = ((bf16[32,256,128]{2,1,0:T(8,128)(2,1)}), bf16[32,256,128]{2,1,0:T(8,128)(2,1)}, u32[]{:S(2)}, u32[]{:S(2)}) async-start(bf16[32,256,128]{2,1,0:T(8,128)(2,1)} %copy.62), calls=%async_computation | async-start | bytes 4194304 | tf_op jit(solution)/shard_map/all_to_all | solution.py:45
  92.3 46.3 %all-to-all-done = bf16[32,256,128]{2,1,0:T(8,128)(2,1)} async-done(((bf16[32,256,128]{2,1,0:T(8,128)(2,1)}), bf16[32,256,128]{2,1,0:T(8,128)(2,1)}, u32[]{:S(2)}, u32[]{:S(2)}) %all-to-all-start) | async-done | bytes 2097184 | tf_op jit(solution)/shard_map/all_to_all | solution.py:45
  138.6 2.8 fusion.99
  141.4 1.9 fusion.39
  143.3 43.1 %all-gather.3.cloned.1.call-done = bf16[352,4096]{1,0:T(8,128)(2,1)} async-done(((bf16[352,128]{1,0:T(8,128)(2,1)}), bf16[352,4096]{1,0:T(8,128)(2,1)}) %all-gather.3.cloned.1.call-update) | async-done | bytes 2883600 | tf_op jit(solution)/shard_map/all_gather | solution.py:30
  186.4 2.3 fusion.51
  192.0 3.8 copy.66
  195.8 7.3 %all-to-all-start.2 = ((bf16[2,4096,128]{2,0,1:T(2,128)(2,1)}), bf16[2,4096,128]{2,0,1:T(2,128)(2,1)S(1)}, u32[]{:S(2)}, u32[]{:S(2)}) async-start(bf16[2,4096,128]{2,0,1:T(2,128)(2,1)} %copy.66), calls=%async_computation.2 | async-start | bytes 4194304 | tf_op jit(solution)/shard_map/all_to_all | solution.py:79
  203.3 1.8 convolution_convert_fusion.1
  205.6 1.8 pad_maximum_fusion
  207.4 4.6 %copy.95 = bf16[352,4096]{0,1:T(8,128)(2,1)} copy(bf16[352,4096]{1,0:T(8,128)(2,1)} %pad_maximum_fusion) | data formatting | bytes 5767168
  212.0 2.1 fusion.2
  214.2 2.1 fusion.3
  216.5 18.1 %copy.70 = bf16[2,4096,128]{2,0,1:T(2,128)(2,1)} copy(bf16[2,4096,128]{2,1,0:T(8,128)(2,1)S(1)} %pad_maximum_fusion.2) | data formatting | bytes 4194304 | tf_op jit(solution)/shard_map/stack | solution.py:61
  234.6 15.8 %all-to-all-done.2 = bf16[2,4096,128]{2,0,1:T(2,128)(2,1)S(1)} async-done(((bf16[2,4096,128]{2,0,1:T(2,128)(2,1)}), bf16[2,4096,128]{2,0,1:T(2,128)(2,1)S(1)}, u32[]{:S(2)}, u32[]{:S(2)}) %all-to-all-start.2) | async-done | bytes 2097184 | tf_op jit(solution)/shard_map/all_to_all | solution.py:79
  250.4 6.5 %all-to-all-start.3 = ((bf16[2,4096,128]{2,0,1:T(2,128)(2,1)}), bf16[2,4096,128]{2,0,1:T(2,128)(2,1)}, u32[]{:S(2)}, u32[]{:S(2)}) async-start(bf16[2,4096,128]{2,0,1:T(2,128)(2,1)} %copy.70), calls=%async_computation.3 | async-start | bytes 4194304 | tf_op jit(solution)/shard_map/all_to_all | solution.py:80
  257.0 1.8 copy.79
  258.8 1.9 copy.93
  260.7 43.8 %all-to-all-done.3 = bf16[2,4096,128]{2,0,1:T(2,128)(2,1)} async-done(((bf16[2,4096,128]{2,0,1:T(2,128)(2,1)}), bf16[2,4096,128]{2,0,1:T(2,128)(2,1)}, u32[]{:S(2)}, u32[]{:S(2)}) %all-to-all-start.3) | async-done | bytes 2097184 | tf_op jit(solution)/shard_map/all_to_all | solution.py:80
  304.5 2.3 copy.94
  307.0 2.0 fusion.54
  310.4 1.9 fusion.18
  313.6 3.5 fusion.21
  318.6 98.9 %psum.7 = f32[16,2,16]{2,1,0:T(2,128)S(1)} all-reduce(f32[16,2,16]{2,1,0:T(2,128)S(1)} %bitcast.141), channel_id=1, replica_groups=mesh['dp'=16,'tensor'=32] {'dp','tensor'}, use_global_device_ids=true, to_apply=%region_1.2 | all-reduce | flops 512 | bytes 4096 | tf_op jit(solution)/shard_map/psum | solution.py:106
  418.1 19.6 %reduce-scatter.4.cloned.1.call-done = bf16[128,352]{1,0:T(8,128)(2,1)} async-done(((bf16[4096,352]{1,0:T(8,128)(2,1)}), bf16[128,352]{1,0:T(8,128)(2,1)}) %reduce-scatter.4.cloned.1.call-update) | async-done | bytes 90128
  (40 shorter events, 15.2 us)
Async XLA Ops:
  7.2 134.2 %all-gather.5.cloned.1.call-start = ((), (), s32[]{:S(2)}) async-start(), calls=%async_computation.6 | async-start | bytes 2973696 | tf_op jit(solution)/shard_map/all_gather | solution.py:29
  33.4 4.5 %copy-start.7 = (bf16[352,128]{1,0:T(8,128)(2,1)S(1)}, bf16[352,128]{1,0:T(8,128)(2,1)}, u32[]{:S(2)}) copy-start(bf16[352,128]{1,0:T(8,128)(2,1)} %param.7) | copy-start | bytes 270340
  33.4 51.2 %all-to-all-start.1 = ((bf16[32,256,128]{2,1,0:T(8,128)(2,1)}), bf16[32,256,128]{2,1,0:T(8,128)(2,1)S(1)}, u32[]{:S(2)}, u32[]{:S(2)}) async-start(bf16[32,256,128]{2,1,0:T(8,128)(2,1)} %copy.65), calls=%async_computation.1 | async-start | bytes 4194304 | tf_op jit(solution)/shard_map/all_to_all | solution.py:44
  37.1 149.3 %all-gather.3.cloned.1.call-start = ((), (), s32[]{:S(2)}) async-start(), calls=%async_computation.5 | async-start | bytes 2973696 | tf_op jit(solution)/shard_map/all_gather | solution.py:30
  84.5 54.1 %all-to-all-start = ((bf16[32,256,128]{2,1,0:T(8,128)(2,1)}), bf16[32,256,128]{2,1,0:T(8,128)(2,1)}, u32[]{:S(2)}, u32[]{:S(2)}) async-start(bf16[32,256,128]{2,1,0:T(8,128)(2,1)} %copy.62), calls=%async_computation | async-start | bytes 4194304 | tf_op jit(solution)/shard_map/all_to_all | solution.py:45
  138.6 2.8 copy-start.1
  186.4 2.6 copy-start.3
  189.0 1.8 copy-start.2
  195.8 54.7 %all-to-all-start.2 = ((bf16[2,4096,128]{2,0,1:T(2,128)(2,1)}), bf16[2,4096,128]{2,0,1:T(2,128)(2,1)S(1)}, u32[]{:S(2)}, u32[]{:S(2)}) async-start(bf16[2,4096,128]{2,0,1:T(2,128)(2,1)} %copy.66), calls=%async_computation.2 | async-start | bytes 4194304 | tf_op jit(solution)/shard_map/all_to_all | solution.py:79
  203.1 234.7 %reduce-scatter.4.cloned.1.call-start = ((), (), s32[]{:S(2)}) async-start(), calls=%async_computation.7 | async-start | bytes 3244032
  234.6 22.4 %copy-start = (bf16[16,128,256]{2,1,0:T(8,128)(2,1)S(1)}, bf16[16,128,256]{2,1,0:T(8,128)(2,1)}, u32[]{:S(2)}) copy-start(bf16[16,128,256]{2,1,0:T(8,128)(2,1)} %param.11) | copy-start | bytes 3145732
  250.4 54.0 %all-to-all-start.3 = ((bf16[2,4096,128]{2,0,1:T(2,128)(2,1)}), bf16[2,4096,128]{2,0,1:T(2,128)(2,1)}, u32[]{:S(2)}, u32[]{:S(2)}) async-start(bf16[2,4096,128]{2,0,1:T(2,128)(2,1)} %copy.70), calls=%async_computation.3 | async-start | bytes 4194304 | tf_op jit(solution)/shard_map/all_to_all | solution.py:80
  304.5 2.3 copy-start.4
  304.5 2.5 copy-start.5
  306.7 2.3 copy-start.6
Sparse Core Ops, SparseCore 0:
  11.0 88.2 all-gather.4
  103.0 83.3 all-gather.2
  212.1 225.5 reduce-scatter.3
where the time goes:
time: 447 us; the launch traced here: 446 us
  waiting for transfers between devices  210 us (47%)
  blocking collectives  119 us (27%)
  local copies, waits for them, and re-layouts  48.7 us (11%)
  matrix products  26.5 us (6%)
  starting transfers between devices  24.5 us (5%)
  between operations  14.6 us (3%)
    psum x1, blocking collectives, body(): totals = lax.psum(table, ('dp', 'tensor'))  98.9 us
    all_to_all x1, waiting for transfers between devices, body(): lax.all_to_all(local_down, 'dp', split_axis=0, concat_axis=1, tiled=True)  46.3 us
    all_to_all x1, waiting for transfers between devices, body(): lax.all_to_all(down_stack, 'dp', split_axis=1, concat_axis=0, tiled=True)  43.8 us
    all_gather x1, waiting for transfers between devices, body(): lax.all_gather(masked, 'tensor', axis=1, tiled=True)  43.1 us
    all_to_all x1, waiting for transfers between devices, body(): lax.all_to_all(local_up, 'dp', split_axis=0, concat_axis=1, tiled=True)  40.2 us
    unnamed x4, waiting for transfers between devices  20.4 us
    all_gather x1, blocking collectives, body(): all_routes = lax.all_gather(routes, 'dp', axis=0, tiled=True)  20.2 us
    another operation x1, local copies, waits for them, and re-layouts, body(): down_stack = jnp.stack(down_terms, axis=0)  18.1 us
  transfers between devices with their start and end apart: 7, of which 6 were waited for; matrix products, arithmetic and copies ran while one was open for 15% of the time, Pallas kernels for 0%

commit v1 on v0

--- a/solution.py
+++ b/solution.py
@@ -103,7 +103,7 @@
         "kdh,ehd->ke", recv_down, down_weight, preferred_element_type=jnp.float32
     )
     table = inner_sums.reshape(all_routes.shape)
-    totals = lax.psum(table, ("dp", "tensor"))
+    totals = jnp.sum(lax.all_gather(table, ("dp", "tensor")), axis=0)
     route_grad = lax.dynamic_slice_in_dim(totals, lax.axis_index("dp"), 1, 0)
     return (summed, up_grad, down_grad, route_grad)
 

time: 447 us -> 581 us (1.30)
  the two profiles are of different devices: /device:TPU:8 before, /device:TPU:1 now
where the time goes in v1:
time: 581 us; the launch traced here: 580 us
  waiting for transfers between devices  438 us (75%)
  local copies, waits for them, and re-layouts  48.1 us (8%)
  matrix products  27 us (5%)
  starting transfers between devices  24.2 us (4%)
  blocking collectives  20.9 us (4%)
  between operations  14.7 us (3%)
  other arithmetic  6.91 us (1%)
    all_gather x1, waiting for transfers between devices, body(): totals = jnp.sum(lax.all_gather(table, ('dp', 'tensor')), axis=0)  135 us
    unnamed x5, waiting for transfers between devices  112 us
    all_to_all x1, waiting for transfers between devices, body(): lax.all_to_all(local_up, 'dp', split_axis=0, concat_axis=1, tiled=True)  47.6 us
    all_to_all x1, waiting for transfers between devices, body(): lax.all_to_all(down_stack, 'dp', split_axis=1, concat_axis=0, tiled=True)  45.2 us
    all_to_all x1, waiting for transfers between devices, body(): lax.all_to_all(local_down, 'dp', split_axis=0, concat_axis=1, tiled=True)  43.4 us
    all_gather x1, waiting for transfers between devices, body(): lax.all_gather(masked, 'tensor', axis=1, tiled=True)  37.6 us
    all_gather x1, blocking collectives, body(): all_routes = lax.all_gather(routes, 'dp', axis=0, tiled=True)  20.9 us
    another operation x1, local copies, waits for them, and re-layouts, body(): down_stack = jnp.stack(down_terms, axis=0)  18.1 us
  transfers between devices with their start and end apart: 8, of which 7 were waited for; matrix products, arithmetic and copies ran while one was open for 12% of the time, Pallas kernels for 0%

profile of v1, /device:TPU:1, one launch (start us, length us, event | category | flops | bytes accessed | tf_op | source)
XLA Modules:
  0.0 579.9 jit_solution(2774708037847643910)
XLA Ops:
  9.5 20.9 %all_gather.13 = f32[16,2,16]{2,1,0:T(2,128)S(1)} all-gather(f32[1,2,16]{2,1,0:T(2,128)S(1)} %copy-done.10), channel_id=1, replica_groups=mesh['dp'=16,'tensor'=32] {'dp'}, dimensions={0}, use_global_device_ids=true | all-gather | bytes 2176 | tf_op jit(solution)/shard_map/all_gather | solution.py:32
  30.4 1.9 convolution_convert_fusion.7
  32.3 2.2 copy.87
  34.5 3.8 all-to-all-start
  39.8 1.9 convolution_convert_fusion.6
  41.7 2.2 copy.90
  43.9 43.4 %all-to-all-done = bf16[32,256,128]{2,1,0:T(8,128)(2,1)S(1)} async-done(((bf16[32,256,128]{2,1,0:T(8,128)(2,1)}), bf16[32,256,128]{2,1,0:T(8,128)(2,1)S(1)}, u32[]{:S(2)}, u32[]{:S(2)}) %all-to-all-start) | async-done | bytes 2097184 | tf_op jit(solution)/shard_map/all_to_all | solution.py:45
  87.3 5.0 all-to-all-start.1
  93.7 47.6 %all-to-all-done.1 = bf16[32,256,128]{2,1,0:T(8,128)(2,1)} async-done(((bf16[32,256,128]{2,1,0:T(8,128)(2,1)}), bf16[32,256,128]{2,1,0:T(8,128)(2,1)}, u32[]{:S(2)}, u32[]{:S(2)}) %all-to-all-start.1) | async-done | bytes 2097184 | tf_op jit(solution)/shard_map/all_to_all | solution.py:44
  143.1 2.2 fusion.45
  145.3 2.0 fusion.39
  147.3 37.6 %all-gather.4.cloned.1.call-done = bf16[352,4096]{1,0:T(8,128)(2,1)} async-done(((bf16[352,128]{1,0:T(8,128)(2,1)}), bf16[352,4096]{1,0:T(8,128)(2,1)}) %all-gather.4.cloned.1.call-update) | async-done | bytes 2883600 | tf_op jit(solution)/shard_map/all_gather | solution.py:30
  184.9 2.3 fusion.48
  189.5 3.8 copy.91
  193.3 9.9 %all-to-all-start.2 = ((bf16[2,4096,128]{2,0,1:T(2,128)(2,1)}), bf16[2,4096,128]{2,0,1:T(2,128)(2,1)S(1)}, u32[]{:S(2)}, u32[]{:S(2)}) async-start(bf16[2,4096,128]{2,0,1:T(2,128)(2,1)} %copy.91), calls=%async_computation.2 | async-start | bytes 4194304 | tf_op jit(solution)/shard_map/all_to_all | solution.py:79
  205.7 1.8 pad_maximum_fusion
  207.5 4.7 copy.122
  212.2 2.1 fusion.3
  214.3 2.1 fusion.2
  216.7 18.1 %copy.95 = bf16[2,4096,128]{2,0,1:T(2,128)(2,1)} copy(bf16[2,4096,128]{2,1,0:T(8,128)(2,1)S(1)} %pad_maximum_fusion.2) | data formatting | bytes 4194304 | tf_op jit(solution)/shard_map/stack | solution.py:61
  234.8 17.3 %all-to-all-done.2 = bf16[2,4096,128]{2,0,1:T(2,128)(2,1)S(1)} async-done(((bf16[2,4096,128]{2,0,1:T(2,128)(2,1)}), bf16[2,4096,128]{2,0,1:T(2,128)(2,1)S(1)}, u32[]{:S(2)}, u32[]{:S(2)}) %all-to-all-start.2) | async-done | bytes 2097184 | tf_op jit(solution)/shard_map/all_to_all | solution.py:79
  252.1 5.0 all-to-all-start.3
  257.4 1.8 copy.104
  259.2 1.8 copy.120
  261.0 45.2 %all-to-all-done.3 = bf16[2,4096,128]{2,0,1:T(2,128)(2,1)} async-done(((bf16[2,4096,128]{2,0,1:T(2,128)(2,1)}), bf16[2,4096,128]{2,0,1:T(2,128)(2,1)}, u32[]{:S(2)}, u32[]{:S(2)}) %all-to-all-start.3) | async-done | bytes 2097184 | tf_op jit(solution)/shard_map/all_to_all | solution.py:80
  306.2 2.2 copy.121
  308.7 2.0 fusion.54
  312.8 1.9 fusion.18
  315.9 3.5 fusion.21
  321.0 111.7 %reduce-scatter.4.cloned.1.call-done = bf16[128,352]{1,0:T(8,128)(2,1)} async-done(((bf16[4096,352]{1,0:T(8,128)(2,1)}), bf16[128,352]{1,0:T(8,128)(2,1)}) %reduce-scatter.4.cloned.1.call-update) | async-done | bytes 90128
  434.3 134.6 %all-gather.8.cloned.1.call-done = f32[512,16,2,16]{3,1,2,0:T(8,128)} async-done(((f32[1,16,2,16]{3,1,2,0:T(8,128)}), f32[512,16,2,16]{3,1,2,0:T(8,128)}) %all-gather.8.cloned.1.call-update) | async-done | bytes 1048592 | tf_op jit(solution)/shard_map/all_gather | solution.py:106
  568.8 4.0 reduce_sum.9
  (50 shorter events, 18.9 us)
Async XLA Ops:
  7.2 2.4 copy-start.10
  7.2 135.9 %all-gather.6.cloned.1.call-start = ((), (), s32[]{:S(2)}) async-start(), calls=%async_computation.6 | async-start | bytes 2973696 | tf_op jit(solution)/shard_map/all_gather | solution.py:29
  34.5 4.5 copy-start.9
  34.5 5.3 copy-start.5
  34.5 52.8 %all-to-all-start = ((bf16[32,256,128]{2,1,0:T(8,128)(2,1)}), bf16[32,256,128]{2,1,0:T(8,128)(2,1)S(1)}, u32[]{:S(2)}, u32[]{:S(2)}) async-start(bf16[32,256,128]{2,1,0:T(8,128)(2,1)} %copy.87), calls=%async_computation | async-start | bytes 4194304 | tf_op jit(solution)/shard_map/all_to_all | solution.py:45
  38.3 146.6 %all-gather.4.cloned.1.call-start = ((), (), s32[]{:S(2)}) async-start(), calls=%async_computation.5 | async-start | bytes 2973696 | tf_op jit(solution)/shard_map/all_gather | solution.py:30
  87.3 54.1 %all-to-all-start.1 = ((bf16[32,256,128]{2,1,0:T(8,128)(2,1)}), bf16[32,256,128]{2,1,0:T(8,128)(2,1)}, u32[]{:S(2)}, u32[]{:S(2)}) async-start(bf16[32,256,128]{2,1,0:T(8,128)(2,1)} %copy.90), calls=%async_computation.1 | async-start | bytes 4194304 | tf_op jit(solution)/shard_map/all_to_all | solution.py:44
  143.0 4.3 copy-start.1
  145.3 42.6 %copy-start.8 = (bf16[1,16,256,128]{3,2,0,1:T(8,128)(2,1)S(1)}, bf16[1,16,256,128]{3,2,0,1:T(8,128)(2,1)}, u32[]{:S(2)}) copy-start(bf16[1,16,256,128]{3,2,0,1:T(8,128)(2,1)} %get-tuple-element.26) | copy-start | bytes 3145732
  184.9 2.6 copy-start.3
  184.9 3.4 copy-start.2
  193.3 58.8 %all-to-all-start.2 = ((bf16[2,4096,128]{2,0,1:T(2,128)(2,1)}), bf16[2,4096,128]{2,0,1:T(2,128)(2,1)S(1)}, u32[]{:S(2)}, u32[]{:S(2)}) async-start(bf16[2,4096,128]{2,0,1:T(2,128)(2,1)} %copy.91), calls=%async_computation.2 | async-start | bytes 4194304 | tf_op jit(solution)/shard_map/all_to_all | solution.py:79
  203.2 229.5 %reduce-scatter.4.cloned.1.call-start = ((), (), s32[]{:S(2)}) async-start(), calls=%async_computation.8 | async-start | bytes 3244032
  234.8 22.6 %copy-start = (bf16[16,128,256]{2,1,0:T(8,128)(2,1)S(1)}, bf16[16,128,256]{2,1,0:T(8,128)(2,1)}, u32[]{:S(2)}) copy-start(bf16[16,128,256]{2,1,0:T(8,128)(2,1)} %param.11) | copy-start | bytes 3145732
  252.1 54.0 %all-to-all-start.3 = ((bf16[2,4096,128]{2,0,1:T(2,128)(2,1)}), bf16[2,4096,128]{2,0,1:T(2,128)(2,1)}, u32[]{:S(2)}, u32[]{:S(2)}) async-start(bf16[2,4096,128]{2,0,1:T(2,128)(2,1)} %copy.95), calls=%async_computation.3 | async-start | bytes 4194304 | tf_op jit(solution)/shard_map/all_to_all | solution.py:80
  257.1 311.7 %all-gather.8.cloned.1.call-start = ((), (), s32[]{:S(2)}) async-start(), calls=%async_computation.7 | async-start | bytes 8404992 | tf_op jit(solution)/shard_map/all_gather | solution.py:106
  306.2 2.3 copy-start.4
  306.2 2.5 copy-start.6
  308.4 2.3 copy-start.7
Sparse Core Ops, SparseCore 0:
  11.1 86.7 all-gather.5
  101.5 83.3 all-gather.3
  212.3 220.2 reduce-scatter.3
  437.7 131.0 all-gather.7
